TPU v7x, 32 devices: a whole 2x2x4 slice. The times are simulated.
32 devices in a mesh: rep: 2 (over y), shard: 16 (over z, x, core).
Axes of the slice: x: 2, y: 2, z: 4, core: 2. Of those that a mesh axis runs over, the one named last changes fastest.
Arguments:
- latents: bfloat16 [32, 128, 1152], P(('rep', 'shard')), may hold values from -5 to 5
- cond: float32 [32, 1152], P(('rep', 'shard')), may hold values from -6 to 6
- timesteps: int32 [32], P(('rep', 'shard')), may hold values from 0 to 999
- cotangent: bfloat16 [32, 128, 1152], P(('rep', 'shard')), may hold values from -6 to 6
- w_qkv: float32 [1152, 3456], P('shard'), may hold values from -0.11785113 to 0.11785113
- w_proj: float32 [1152, 1152], P('shard'), may hold values from -0.75 to 0.75
- w_fc1: float32 [1152, 4608], P('shard'), may hold values from -0.1875 to 0.1875
- w_fc2: float32 [4608, 1152], P('shard'), may hold values from -0.1875 to 0.1875
- w_ada: float32 [1152, 6912], P(None, 'shard'), may hold values from -0.015625 to 0.015625
- biases: float32 [16128], replicated, may hold values from -3 to 3
- m_qkv: float32 [1152, 3456], P('shard', 'rep'), may hold values from -0.00012272017 to 0.00012272017
- m_proj: float32 [1152, 1152], P('shard', 'rep'), may hold values from -0.00012272017 to 0.00012272017
- m_fc1: float32 [1152, 4608], P('shard', 'rep'), may hold values from -0.00012272017 to 0.00012272017
- m_fc2: float32 [4608, 1152], P('shard', 'rep'), may hold values from -0.00012272017 to 0.00012272017
- m_ada: float32 [1152, 6912], P('rep', 'shard'), may hold values from -0.00012272017 to 0.00012272017
- m_bias: float32 [16128], replicated, may hold values from -0.00012272017 to 0.00012272017
- v_qkv: float32 [1152, 3456], P('shard', 'rep'), may hold values from 4.1834e-11 to 1.67336e-10
- v_proj: float32 [1152, 1152], P('shard', 'rep'), may hold values from 4.1834e-11 to 1.67336e-10
- v_fc1: float32 [1152, 4608], P('shard', 'rep'), may hold values from 4.1834e-11 to 1.67336e-10
- v_fc2: float32 [4608, 1152], P('shard', 'rep'), may hold values from 4.1834e-11 to 1.67336e-10
- v_ada: float32 [1152, 6912], P('rep', 'shard'), may hold values from 4.1834e-11 to 1.67336e-10
- v_bias: float32 [16128], replicated, may hold values from 4.1834e-11 to 1.67336e-10
Outputs:
- block_out: float32 [32, 128, 1152], P(('rep', 'shard'))
- latents_grad: float32 [32, 128, 1152], P(('rep', 'shard'))
- cond_grad: float32 [32, 1152], P(('rep', 'shard'))
- new_qkv: float32 [1152, 3456], P('shard')
- new_proj: float32 [1152, 1152], P('shard')
- new_fc1: float32 [1152, 4608], P('shard')
- new_fc2: float32 [4608, 1152], P('shard')
- new_ada: float32 [1152, 6912], P(None, 'shard')
- bias_update: float32 [16128], replicated
- new_m_qkv: float32 [1152, 3456], P('shard', 'rep')
- new_m_proj: float32 [1152, 1152], P('shard', 'rep')
- new_m_fc1: float32 [1152, 4608], P('shard', 'rep')
- new_m_fc2: float32 [4608, 1152], P('shard', 'rep')
- new_m_ada: float32 [1152, 6912], P('rep', 'shard')
- new_m_bias: float32 [16128], replicated
- new_v_qkv: float32 [1152, 3456], P('shard', 'rep')
- new_v_proj: float32 [1152, 1152], P('shard', 'rep')
- new_v_fc1: float32 [1152, 4608], P('shard', 'rep')
- new_v_fc2: float32 [4608, 1152], P('shard', 'rep')
- new_v_ada: float32 [1152, 6912], P('rep', 'shard')
- new_v_bias: float32 [16128], replicated
All inputs are finite; a program needn't handle non-finite values.
Results may differ from a plain program's by a relative error of at most 0.014.
Values may be sent and summed in bfloat16 or wider, within the bound.
No kernel may reach another device: no remote copies, remote signals or barrier semaphores. Data moves between devices by JAX's collectives and lax.ppermute only.
A program may use at most 256 MiB of HBM per device.

v0:
```python
import math
import jax
import jax.numpy as jnp
from jax import lax
from jax.sharding import PartitionSpec as P

HD = 72
H = 16
FF = 4608
ln_eps = 1e-06
beta_one = 0.9
beta_two = 0.999
adam_eps = 1e-08
learn_rate = 0.03
decay_rate = 0.01
step_count = 2
gelu_coef = 0.044715


def product(form, left, right):
    return jnp.einsum(form, left, right, preferred_element_type=jnp.float32)


def normalize(rows):
    center = rows - jnp.mean(rows, axis=-1, keepdims=True)
    rstd = lax.rsqrt(jnp.mean(center * center, axis=-1, keepdims=True) + ln_eps)
    return (center * rstd, rstd)


def norm_back(grad, normed, rstd):
    return rstd * (
        grad
        - jnp.mean(grad, axis=-1, keepdims=True)
        - normed * jnp.mean(grad * normed, axis=-1, keepdims=True)
    )


def gelu_parts(pre):
    root = math.sqrt(2.0 / math.pi)
    inner = root * (pre + gelu_coef * pre * pre * pre)
    tangent = jnp.tanh(inner)
    value = 0.5 * pre * (1.0 + tangent)
    slope = 0.5 * (1.0 + tangent) + 0.5 * pre * (1.0 - tangent * tangent) * root * (
        1.0 + 3.0 * gelu_coef * pre * pre
    )
    return (value, slope)


def time_embed(steps, width):
    half = width // 2
    freqs = jnp.exp(-math.log(10000.0) * jnp.arange(half, dtype=jnp.float32) / half)
    angles = steps.astype(jnp.float32)[:, None] * freqs[None, :]
    return jnp.concatenate([jnp.cos(angles), jnp.sin(angles)], axis=1)


def adam_change(weight, grad, first, second, clip):
    scaled = grad * clip
    first_new = beta_one * first + (1.0 - beta_one) * scaled
    second_new = beta_two * second + (1.0 - beta_two) * scaled * scaled
    first_hat = first_new / (1.0 - beta_one**step_count)
    second_hat = second_new / (1.0 - beta_two**step_count)
    change = -learn_rate * (first_hat / (jnp.sqrt(second_hat) + adam_eps) + decay_rate * weight)
    return (change, first_new, second_new)


def shards(
    latents,
    cond,
    timesteps,
    cotangent,
    w_qkv,
    w_proj,
    w_fc1,
    w_fc2,
    w_ada,
    biases,
    m_qkv,
    m_proj,
    m_fc1,
    m_fc2,
    m_ada,
    m_bias,
    v_qkv,
    v_proj,
    v_fc1,
    v_fc2,
    v_ada,
    v_bias,
):
    axes = ("rep", "shard")
    replicas = lax.axis_size("rep")
    parts = lax.axis_size("shard")
    devices = replicas * parts
    rank = lax.axis_index("rep")
    turn = rank % 2
    couples = [(i, i ^ 1) for i in range(replicas)]
    length, width = latents.shape[1:]
    inner = H * HD
    half = inner // 2
    heads = H // 2
    rows = w_qkv.shape[0]
    folds = FF // (2 * width)
    unit = FF // (2 * parts * folds)

    def swap(value):
        return lax.ppermute(value, "rep", couples)

    def ordered(own, other, axis):
        first = jnp.concatenate([own, other], axis=axis)
        second = jnp.concatenate([other, own], axis=axis)
        return jnp.where(turn == 0, first, second)

    def own_half(value, axis):
        count = value.shape[axis] // 2
        return lax.dynamic_slice_in_dim(value, turn * count, count, axis)

    def spread(value):
        copies = jnp.broadcast_to(value, (devices,) + value.shape[1:])
        return lax.all_to_all(copies, axes, split_axis=0, concat_axis=0, tiled=True)

    b_q = own_half(biases[0:inner], 0)
    b_v = own_half(biases[inner : 2 * inner], 0)
    b_proj = biases[2 * inner : 2 * inner + width]
    b_fc1 = biases[2 * inner + width : 2 * inner + width + FF]
    b_fc2 = biases[2 * inner + width + FF : 2 * inner + 2 * width + FF]
    b_ada = biases[biases.shape[0] - 6 * width :]
    units = lax.dynamic_index_in_dim(b_fc1.reshape(parts, 2, folds, unit), turn, 1, keepdims=False)
    b_one = jnp.transpose(units, (1, 0, 2)).reshape(folds, width)
    wq_half = own_half(w_qkv.astype(jnp.bfloat16).reshape(rows, 3, inner), 2)
    pack_attn = jnp.concatenate(
        [w_proj.astype(jnp.bfloat16), wq_half.reshape(rows, 3 * half)], axis=1
    )
    full_attn = lax.all_gather(pack_attn, "shard", axis=0, tiled=True)
    wp_b = full_attn[:, :width]
    wq_b = full_attn[:, width:]
    w1_half = lax.dynamic_index_in_dim(
        w_fc1.astype(jnp.bfloat16).reshape(rows, parts, 2, folds, unit), turn, 2, keepdims=False
    )
    w1_half = jnp.transpose(w1_half, (0, 2, 1, 3)).reshape(rows, folds * width)
    w2_half = own_half(w_fc2.astype(jnp.bfloat16), 0).reshape(folds, rows, width)
    pack_mlp = jnp.concatenate([w1_half] + [w2_half[f] for f in range(folds)], axis=1)
    full_mlp = lax.all_gather(pack_mlp, "shard", axis=0, tiled=True)
    w1_b = [full_mlp[:, f * width : (f + 1) * width] for f in range(folds)]
    w2_b = [full_mlp[:, (folds + f) * width : (folds + f + 1) * width] for f in range(folds)]
    cvec = cond + time_embed(timesteps, width)
    silu_c = jax.nn.silu(cvec).astype(jnp.bfloat16)
    ada_local = w_ada.astype(jnp.bfloat16)
    silu_all = spread(silu_c)
    silu_group = lax.dynamic_slice_in_dim(silu_all, rank * parts, parts, 0)
    mod_cols = jnp.dot(silu_group, ada_local, preferred_element_type=jnp.float32)
    mod = lax.all_to_all(mod_cols, "shard", split_axis=0, concat_axis=1, tiled=True) + b_ada
    shift1, scale1, gate1, shift2, scale2, gate2 = [
        mod[:, i * width : (i + 1) * width] for i in range(6)
    ]
    tokens = latents[0].astype(jnp.float32)
    n_one, r_one = normalize(tokens)
    a_one = (n_one * (1.0 + scale1) + shift1).astype(jnp.bfloat16)
    grad_out = cotangent[0].astype(jnp.float32)
    d_mlp = grad_out * gate2
    d_mlp_b = d_mlp.astype(jnp.bfloat16)
    a_one2 = jnp.concatenate([a_one, swap(a_one)], axis=0)
    d_mlp2 = jnp.concatenate([d_mlp_b, swap(d_mlp_b)], axis=0)
    qkv = product("ld,de->le", a_one2, wq_b)
    shape = (2, length, heads, HD)
    queries = (qkv[:, :half] + b_q).astype(jnp.bfloat16).reshape(shape)
    key_rows = qkv[:, half : 2 * half].astype(jnp.bfloat16).reshape(shape)
    value_rows = (qkv[:, 2 * half :] + b_v).astype(jnp.bfloat16).reshape(shape)
    factor = HD ** (-0.5)
    scores = product("bqhd,bkhd->bhqk", queries, key_rows) * factor
    top = jnp.max(scores, axis=-1, keepdims=True)
    expo = jnp.exp(scores - top)
    probs = expo / jnp.sum(expo, axis=-1, keepdims=True)
    probs_b = probs.astype(jnp.bfloat16)
    heads_out = product("bhqk,bkhd->bqhd", probs_b, value_rows).astype(jnp.bfloat16)
    heads_flat = heads_out.reshape(2, length, half)
    heads_other = swap(heads_flat)[::-1]
    heads_own = ordered(heads_flat[0], heads_other[0], 1)
    attn = product("le,ed->ld", heads_own, wp_b) + b_proj
    x_one = tokens + gate1 * attn
    n_two, r_two = normalize(x_one)
    a_two = (n_two * (1.0 + scale2) + shift2).astype(jnp.bfloat16)
    a_two2 = jnp.concatenate([a_two, swap(a_two)], axis=0)
    mlp_sum = 0.0
    d_a2_sum = 0.0
    g_one = []
    g_two = []
    g_b_one = []
    for f in range(folds):
        pre = product("ld,df->lf", a_two2, w1_b[f]) + b_one[f]
        act_val, act_slope = gelu_parts(pre)
        act = act_val.astype(jnp.bfloat16)
        mlp_sum = mlp_sum + product("lf,fd->ld", act, w2_b[f])
        d_pre = product("ld,fd->lf", d_mlp2, w2_b[f]) * act_slope
        d_pre_b = d_pre.astype(jnp.bfloat16)
        d_a2_sum = d_a2_sum + product("lf,df->ld", d_pre_b, w1_b[f])
        g_one.append(product("ld,lf->df", a_two2, d_pre_b).astype(jnp.bfloat16))
        g_two.append(product("lf,ld->fd", act, d_mlp2).astype(jnp.bfloat16))
        g_b_one.append(jnp.sum(d_pre, axis=0))
    grads_mlp = lax.psum_scatter(
        jnp.concatenate(g_one + g_two, axis=1), "shard", scatter_dimension=0, tiled=True
    )
    d_a2 = d_a2_sum[:length] + swap(d_a2_sum[length:].astype(jnp.bfloat16)).astype(jnp.float32)
    mlp = mlp_sum[:length] + swap(mlp_sum[length:].astype(jnp.bfloat16)).astype(jnp.float32) + b_fc2
    block_out = (x_one + gate2 * mlp)[None]
    d_gate2 = jnp.sum(grad_out * mlp, axis=0)
    g_b_fc2 = jnp.sum(d_mlp, axis=0)
    d_shift2 = jnp.sum(d_a2, axis=0)
    d_scale2 = jnp.sum(d_a2 * n_two, axis=0)
    dx_one = grad_out + norm_back(d_a2 * (1.0 + scale2), n_two, r_two)
    d_gate1 = jnp.sum(dx_one * attn, axis=0)
    d_attn = dx_one * gate1
    d_attn_b = d_attn.astype(jnp.bfloat16)
    g_b_proj = jnp.sum(d_attn, axis=0)
    d_attn2 = jnp.concatenate([d_attn_b, swap(d_attn_b)], axis=0)
    d_heads = product("ld,ed->le", d_attn2, own_half(wp_b, 0)).astype(jnp.bfloat16).reshape(shape)
    heads_all = jnp.concatenate([heads_own, ordered(heads_flat[1], heads_other[1], 1)], axis=0)
    g_proj = product("le,ld->ed", heads_all, own_half(d_attn2, 1)).astype(jnp.bfloat16)
    delta = jnp.sum(d_heads.astype(jnp.float32) * heads_out.astype(jnp.float32), axis=-1)
    delta = jnp.transpose(delta, (0, 2, 1))[..., None]
    d_probs = product("bqhd,bkhd->bhqk", d_heads, value_rows)
    d_scores = (probs * (d_probs - delta) * factor).astype(jnp.bfloat16)
    d_q = product("bhqk,bkhd->bqhd", d_scores, key_rows)
    d_k = product("bhqk,bqhd->bkhd", d_scores, queries)
    d_v = product("bhqk,bqhd->bkhd", probs_b, d_heads)
    g_b_q = jnp.sum(d_q, axis=(0, 1)).reshape(half)
    g_b_v = jnp.sum(d_v, axis=(0, 1)).reshape(half)
    d_qkv = jnp.concatenate(
        [piece.astype(jnp.bfloat16).reshape(2 * length, half) for piece in (d_q, d_k, d_v)], axis=1
    )
    g_qkv = product("ld,le->de", a_one2, d_qkv).astype(jnp.bfloat16)
    grads_attn = lax.psum_scatter(
        jnp.concatenate([g_proj, g_qkv], axis=1), "shard", scatter_dimension=0, tiled=True
    )
    d_a1_sum = product("le,de->ld", d_qkv, wq_b)
    d_a1 = d_a1_sum[:length] + swap(d_a1_sum[length:].astype(jnp.bfloat16)).astype(jnp.float32)
    d_shift1 = jnp.sum(d_a1, axis=0)
    d_scale1 = jnp.sum(d_a1 * n_one, axis=0)
    latents_grad = (dx_one + norm_back(d_a1 * (1.0 + scale1), n_one, r_one))[None]
    d_mod = jnp.concatenate([d_shift1, d_scale1, d_gate1, d_shift2, d_scale2, d_gate2])
    d_mod_b = d_mod.astype(jnp.bfloat16).reshape(1, parts, d_mod.shape[0] // parts)
    d_mod_b = jnp.broadcast_to(d_mod_b, (replicas,) + d_mod_b.shape[1:])
    d_mod_cols = lax.all_to_all(
        d_mod_b.reshape(devices, d_mod_b.shape[2]), axes, split_axis=0, concat_axis=0, tiled=True
    )
    g_ada = jnp.dot(silu_all.T, d_mod_cols, preferred_element_type=jnp.float32)
    group_cols = lax.dynamic_slice_in_dim(d_mod_cols, rank * parts, parts, 0)
    silu_terms = jnp.dot(group_cols, ada_local.T, preferred_element_type=jnp.float32)
    silu_terms = lax.all_to_all(silu_terms, "shard", split_axis=0, concat_axis=0, tiled=True)
    silu_grad = jnp.sum(silu_terms, axis=0, keepdims=True)
    sig = jax.nn.sigmoid(cvec)
    cond_grad = silu_grad * sig * (1.0 + cvec * (1.0 - sig))
    mine = jnp.arange(2) == turn
    units_one = jnp.transpose(jnp.stack(g_b_one).reshape(folds, parts, unit), (1, 0, 2))
    bias_partial = jnp.concatenate(
        [
            jnp.where(mine[:, None], g_b_q[None], 0.0).reshape(inner),
            jnp.where(mine[:, None], g_b_v[None], 0.0).reshape(inner),
            g_b_proj,
            jnp.where(mine[None, :, None, None], units_one[:, None], 0.0).reshape(FF),
            g_b_fc2,
            d_mod,
        ]
    )
    chunk = bias_partial.shape[0] // devices
    bias_terms = lax.all_to_all(
        bias_partial.reshape(devices, chunk), axes, split_axis=0, concat_axis=0, tiled=True
    )
    bias_chunk = jnp.sum(bias_terms, axis=0)

    def complete(own):
        return swap(own) if replicas == 2 else jnp.zeros_like(own)

    def share(own, axis):
        if replicas == 2:
            return own
        return lax.psum_scatter(own.astype(jnp.float32), "rep", scatter_dimension=axis, tiled=True)

    def split(value):
        if replicas == 2:
            return own_half(value, 1)
        return share(value, 1)

    own_proj = grads_attn[:, :half]
    if replicas > 2:
        own_proj = share(ordered(own_proj, jnp.zeros_like(own_proj), 1), 1)
    own_qkv = grads_attn[:, half:].reshape(rows, 3, half)
    full_qkv = ordered(own_qkv, complete(own_qkv), 2).reshape(rows, 3 * inner)
    own_mlp = grads_mlp[:, None]
    full_mlp_grad = ordered(own_mlp, complete(own_mlp), 1)
    full_one = full_mlp_grad[:, :, : folds * width].reshape(rows, 2, folds, parts, unit)
    full_one = jnp.transpose(full_one, (0, 3, 1, 2, 4)).reshape(rows, FF)
    full_two = full_mlp_grad[:, :, folds * width :].reshape(rows, 2, folds, width)
    full_two = jnp.transpose(full_two, (1, 2, 0, 3)).reshape(2 * folds * rows, width)
    count_ada = width // replicas
    own_ada = lax.dynamic_slice_in_dim(g_ada, rank * count_ada, count_ada, 0)
    pieces = [split(full_qkv), own_proj, split(full_one), split(full_two), own_ada]
    pieces = [piece.astype(jnp.float32) for piece in pieces]
    if replicas == 2:
        counted = [grads_attn.astype(jnp.float32), grads_mlp.astype(jnp.float32), own_ada]
    else:
        counted = pieces
    squares = sum((jnp.sum(p * p) for p in counted)) + jnp.sum(bias_chunk * bias_chunk)
    totals = spread(jnp.concatenate([bias_chunk, squares[None]])[None])
    g_bias = totals[:, :chunk].reshape(devices * chunk)
    gnorm = jnp.sqrt(jnp.sum(totals[:, chunk]))
    clip = 1.0 / jnp.maximum(gnorm, 1.0)
    weights = (w_qkv, w_proj, w_fc1, w_fc2, w_ada)
    dims = (1, 1, 1, 1, 0)
    firsts = (m_qkv, m_proj, m_fc1, m_fc2, m_ada)
    seconds = (v_qkv, v_proj, v_fc1, v_fc2, v_ada)
    new_w = []
    new_m = []
    new_v = []
    for weight, dim, grad, first, second in zip(weights, dims, pieces, firsts, seconds):
        count = weight.shape[dim] // replicas
        own = lax.dynamic_slice_in_dim(weight, rank * count, count, dim)
        change, first_new, second_new = adam_change(own, grad, first, second, clip)
        change = change.astype(jnp.bfloat16)
        if replicas == 2:
            changes = ordered(change, swap(change), dim)
        else:
            changes = lax.all_gather(change, "rep", axis=dim, tiled=True)
        new_w.append(weight + changes.astype(jnp.float32))
        new_m.append(first_new)
        new_v.append(second_new)
    bias_update, new_m_bias, new_v_bias = adam_change(biases, g_bias, m_bias, v_bias, clip)
    return (
        block_out,
        latents_grad,
        cond_grad,
        *new_w,
        bias_update,
        *new_m,
        new_m_bias,
        *new_v,
        new_v_bias,
    )


def solution(mesh):
    in_specs = (
        P(("rep", "shard"), None, None),
        P(("rep", "shard"), None),
        P(("rep", "shard")),
        P(("rep", "shard"), None, None),
        P("shard", None),
        P("shard", None),
        P("shard", None),
        P("shard", None),
        P(None, "shard"),
        P(),
        P("shard", "rep"),
        P("shard", "rep"),
        P("shard", "rep"),
        P("shard", "rep"),
        P("rep", "shard"),
        P(),
        P("shard", "rep"),
        P("shard", "rep"),
        P("shard", "rep"),
        P("shard", "rep"),
        P("rep", "shard"),
        P(),
    )
    out_specs = (
        P(("rep", "shard"), None, None),
        P(("rep", "shard"), None, None),
        P(("rep", "shard"), None),
        P("shard", None),
        P("shard", None),
        P("shard", None),
        P("shard", None),
        P(None, "shard"),
        P(),
        P("shard", "rep"),
        P("shard", "rep"),
        P("shard", "rep"),
        P("shard", "rep"),
        P("rep", "shard"),
        P(),
        P("shard", "rep"),
        P("shard", "rep"),
        P("shard", "rep"),
        P("shard", "rep"),
        P("rep", "shard"),
        P(),
    )
    return jax.shard_map(shards, mesh=mesh, in_specs=in_specs, out_specs=out_specs, check_vma=False)
```

profile of v0, /device:TPU:0, one launch (start us, length us, event | category | flops | bytes accessed | tf_op | source)
XLA Modules:
  0.0 525.0 jit_solution(11382499632518451920)
XLA Ops:
  20.7 7.3 %all-to-all-start = ((bf16[32,2,576]{2,1,0:T(2,128)(2,1)}), bf16[32,2,576]{2,1,0:T(2,128)(2,1)S(1)}, u32[]{:S(2)}, u32[]{:S(2)}) async-start(bf16[32,2,576]{2,1,0:T(2,128)(2,1)} %reshape.315), calls=%async_computation | async-start | bytes 163840 | tf_op jit(solution)/shard_map/all_to_all | solution.py:119
  28.5 8.4 %all-to-all-done = bf16[32,2,576]{2,1,0:T(2,128)(2,1)S(1)} async-done(((bf16[32,2,576]{2,1,0:T(2,128)(2,1)}), bf16[32,2,576]{2,1,0:T(2,128)(2,1)S(1)}, u32[]{:S(2)}, u32[]{:S(2)}) %all-to-all-start) | async-done | bytes 73760 | tf_op jit(solution)/shard_map/all_to_all | solution.py:119
  38.2 3.7 all-to-all-start.1
  42.3 6.2 %all-to-all-done.1 = f32[16,1,432]{2,1,0:T(1,128)S(1)} async-done(((f32[16,1,432]{2,1,0:T(1,128)}), f32[16,1,432]{2,1,0:T(1,128)S(1)}, u32[]{:S(2)}, u32[]{:S(2)}) %all-to-all-start.1) | async-done | bytes 27680 | tf_op jit(solution)/shard_map/all_to_all | solution.py:151
  50.1 7.9 %collective-permute-done = bf16[128,1152]{1,0:T(8,128)(2,1)S(1)} collective-permute-done((bf16[128,1152]{1,0:T(8,128)(2,1)S(1)}, bf16[128,1152]{1,0:T(8,128)(2,1)S(1)}, u32[]{:S(2)}, u32[]{:S(2)}) %collective-permute-start) | collective-permute-done | bytes 294944 | tf_op jit(solution)/shard_map/ppermute | solution.py:106
  57.9 21.5 %all-gather.3.cloned.1.call-done = bf16[1152,2880]{1,0:T(8,128)(2,1)} async-done(((bf16[72,2880]{1,0:T(8,128)(2,1)}), bf16[1152,2880]{1,0:T(8,128)(2,1)}) %all-gather.3.cloned.1.call-update) | async-done | bytes 6635536 | tf_op jit(solution)/shard_map/all_gather | solution.py:133
  79.4 4.0 fusion.3
  89.5 6.8 %collective-permute-done.1 = bf16[2,128,576]{1,2,0:T(8,128)(2,1)S(1)} collective-permute-done((bf16[2,128,576]{1,2,0:T(8,128)(2,1)S(1)}, bf16[2,128,576]{1,2,0:T(8,128)(2,1)S(1)}, u32[]{:S(2)}, u32[]{:S(2)}) %collective-permute-start.1) | collective-permute-done | bytes 294944 | tf_op jit(solution)/shard_map/ppermute | solution.py:106
  97.1 3.3 fusion.121
  103.7 7.1 %collective-permute-done.2 = bf16[128,1152]{1,0:T(8,128)(2,1)S(1)} collective-permute-done((bf16[128,1152]{1,0:T(8,128)(2,1)S(1)}, bf16[128,1152]{1,0:T(8,128)(2,1)S(1)}, u32[]{:S(2)}, u32[]{:S(2)}) %collective-permute-start.2) | collective-permute-done | bytes 294944 | tf_op jit(solution)/shard_map/ppermute | solution.py:106
  110.8 58.5 %all-gather.5.cloned.1.call-done = bf16[1152,4608]{1,0:T(8,128)(2,1)} async-done(((bf16[72,4608]{1,0:T(8,128)(2,1)}), bf16[1152,4608]{1,0:T(8,128)(2,1)}) %all-gather.5.cloned.1.call-update) | async-done | bytes 10616848 | tf_op jit(solution)/shard_map/all_gather | solution.py:142
  172.3 3.9 convolution_add_fusion.2
  189.4 5.2 collective-permute-done.5
  195.4 4.7 collective-permute-done.3
  204.6 6.0 %collective-permute-done.6 = bf16[128,1152]{1,0:T(8,128)(2,1)S(1)} collective-permute-done((bf16[128,1152]{1,0:T(8,128)(2,1)S(1)}, bf16[128,1152]{1,0:T(8,128)(2,1)S(1)}, u32[]{:S(2)}, u32[]{:S(2)}) %collective-permute-start.6) | collective-permute-done | bytes 294944 | tf_op jit(solution)/shard_map/ppermute | solution.py:106
  224.1 8.6 %copy.290 = bf16[1152,2304]{1,0:T(8,128)(2,1)} copy(bf16[1152,2304]{0,1:T(8,128)(2,1)} %pad_maximum_fusion.1) | data formatting | bytes 10616832
  241.7 28.2 %pad_maximum_fusion = bf16[1152,4608]{0,1:T(8,128)(2,1)} fusion(bf16[1152,1152]{0,1:T(8,128)(2,1)S(1)} %convolution_convert_fusion, bf16[1152,1152]{0,1:T(8,128)(2,1)S(1)} %convolution_convert_fusion.1, bf16[1152,1152]{0,1:T(8,128)(2,1)S(1)} %convolution_convert_fusion.2, bf16[1152,1152]{0,1:T(8,128)(2,1)S(1)} %convolution_convert_fusion.3), kind=kLoop, calls=%fused_computation.1 | loop fusion | flops 42467328 | bytes 21233664 | tf_op jit(solution)/shard_map/concatenate | solution.py:200
  269.8 15.4 %copy.292 = bf16[1152,4608]{1,0:T(8,128)(2,1)} copy(bf16[1152,4608]{0,1:T(8,128)(2,1)} %pad_maximum_fusion) | data formatting | bytes 21233664
  290.6 4.0 fusion.1
  316.6 4.3 all-to-all-done.2
  324.5 6.3 %all-to-all-done.4 = f32[32,1,504]{2,1,0:T(1,128)S(1)} async-done(((f32[32,1,504]{2,1,0:T(1,128)}), f32[32,1,504]{2,1,0:T(1,128)S(1)}, u32[]{:S(2)}, u32[]{:S(2)}) %all-to-all-start.4) | async-done | bytes 64544 | tf_op jit(solution)/shard_map/all_to_all | solution.py:265
  330.8 3.5 all-to-all-start.3
  337.7 3.5 all-to-all-done.3
  345.3 87.4 %reduce-scatter.9.cloned.1.call-done = bf16[72,4608]{1,0:T(8,128)(2,1)} async-done(((bf16[1152,4608]{1,0:T(8,128)(2,1)}), bf16[72,4608]{1,0:T(8,128)(2,1)}) %reduce-scatter.9.cloned.1.call-update) | async-done | bytes 663568
  438.8 4.6 all-to-all-start.5
  453.7 3.1 multiply_convert_fusion.6
  460.8 3.9 multiply_convert_fusion.2
  471.1 3.3 collective-permute-done.10
  489.9 5.0 reshape.287
  499.7 3.5 convert_add_fusion
  505.0 3.2 multiply_convert_fusion.3
  510.9 5.9 %collective-permute-done.13 = bf16[288,576]{1,0:T(8,128)(2,1)S(1)} collective-permute-done((bf16[288,576]{1,0:T(8,128)(2,1)S(1)}, bf16[288,576]{1,0:T(8,128)(2,1)S(1)}, u32[]{:S(2)}, u32[]{:S(2)}) %collective-permute-start.13) | collective-permute-done | bytes 331808 | tf_op jit(solution)/shard_map/ppermute | solution.py:106
  (348 shorter events, 157.3 us)
Async XLA Ops:
  7.2 72.2 %all-gather.3.cloned.1.call-start = ((), (), s32[]{:S(2)}) async-start(), calls=%async_computation.8 | async-start | bytes 7206912 | tf_op jit(solution)/shard_map/all_gather | solution.py:133
  10.3 159.0 %all-gather.5.cloned.1.call-start = ((), (), s32[]{:S(2)}) async-start(), calls=%async_computation.9 | async-start | bytes 11280384 | tf_op jit(solution)/shard_map/all_gather | solution.py:142
  16.6 20.6 %copy-start = (f32[1152,432]{0,1:T(8,128)S(1)}, f32[1152,432]{0,1:T(8,128)}, u32[]{:S(2)}) copy-start(f32[1152,432]{0,1:T(8,128)} %param.30) | copy-start | bytes 5971972
  20.7 16.2 %all-to-all-start = ((bf16[32,2,576]{2,1,0:T(2,128)(2,1)}), bf16[32,2,576]{2,1,0:T(2,128)(2,1)S(1)}, u32[]{:S(2)}, u32[]{:S(2)}) async-start(bf16[32,2,576]{2,1,0:T(2,128)(2,1)} %reshape.315), calls=%async_computation | async-start | bytes 163840 | tf_op jit(solution)/shard_map/all_to_all | solution.py:119
  28.2 20.7 %copy-start.55 = (f32[128]{0:T(128)}, f32[128]{0:T(128)S(1)}, u32[]{:S(2)}) copy-start(f32[128]{0:T(128)S(1)} %broadcast_multiply_fusion.5) | copy-start | bytes 1540
  38.2 10.4 %all-to-all-start.1 = ((f32[16,1,432]{2,1,0:T(1,128)}), f32[16,1,432]{2,1,0:T(1,128)S(1)}, u32[]{:S(2)}, u32[]{:S(2)}) async-start(f32[16,1,432]{2,1,0:T(1,128)} %copy.246), calls=%async_computation.1 | async-start | bytes 65536 | tf_op jit(solution)/shard_map/all_to_all | solution.py:151
  41.9 300.0 %reduce-scatter.7.cloned.1.call-start = ((), (), s32[]{:S(2)}) async-start(), calls=%async_computation.10 | async-start | bytes 5640192
  49.2 34.3 %copy-start.19 = (bf16[128,1152]{1,0:T(8,128)(2,1)}, bf16[128,1152]{1,0:T(8,128)(2,1)S(1)}, u32[]{:S(2)}) copy-start(bf16[128,1152]{1,0:T(8,128)(2,1)S(1)} %fusion.50) | copy-start | bytes 884740
  49.2 8.8 %collective-permute-start = (bf16[128,1152]{1,0:T(8,128)(2,1)S(1)}, bf16[128,1152]{1,0:T(8,128)(2,1)S(1)}, u32[]{:S(2)}, u32[]{:S(2)}) collective-permute-start(bf16[128,1152]{1,0:T(8,128)(2,1)S(1)} %fusion.50), channel_id=1, source_target_pairs={{0,16},{16,0},{1,17},{17,1},{2,18},{18,2},{3,19},{19,3},{4,20},{20... | collective-permute-start | bytes 884744 | tf_op jit(solution)/shard_map/ppermute | solution.py:106
  57.9 21.5 %copy-start.43 = (bf16[128,1152]{1,0:T(8,128)(2,1)}, bf16[128,1152]{1,0:T(8,128)(2,1)S(1)}, u32[]{:S(2)}) copy-start(bf16[128,1152]{1,0:T(8,128)(2,1)S(1)} %collective-permute-done) | copy-start | bytes 884740
  87.1 9.2 %collective-permute-start.1 = (bf16[2,128,576]{1,2,0:T(8,128)(2,1)S(1)}, bf16[2,128,576]{1,2,0:T(8,128)(2,1)S(1)}, u32[]{:S(2)}, u32[]{:S(2)}) collective-permute-start(bf16[2,128,576]{1,2,0:T(8,128)(2,1)S(1)} %bitcast.156), channel_id=1, source_target_pairs={{0,16},{16,0},{1,17},{17,1},{2,18},{18,2},{3,19},{19,3},{4,20},{20... | collective-permute-start | bytes 884744 | tf_op jit(solution)/shard_map/ppermute | solution.py:106
  100.8 71.4 %copy-start.10 = (bf16[128,1152]{1,0:T(8,128)(2,1)}, bf16[128,1152]{1,0:T(8,128)(2,1)S(1)}, u32[]{:S(2)}) copy-start(bf16[128,1152]{1,0:T(8,128)(2,1)S(1)} %add_convert_fusion) | copy-start | bytes 884740
  100.8 9.9 %collective-permute-start.2 = (bf16[128,1152]{1,0:T(8,128)(2,1)S(1)}, bf16[128,1152]{1,0:T(8,128)(2,1)S(1)}, u32[]{:S(2)}, u32[]{:S(2)}) collective-permute-start(bf16[128,1152]{1,0:T(8,128)(2,1)S(1)} %add_convert_fusion), channel_id=1, source_target_pairs={{0,16},{16,0},{1,17},{17,1},{2,18},{18,2},{3,19},{19,3},{4,20},{20... | collective-permute-start | bytes 884744 | tf_op jit(solution)/shard_map/ppermute | solution.py:106
  103.1 73.0 %collective-permute-start.4 = (bf16[128,1152]{1,0:T(8,128)(2,1)}, bf16[128,1152]{1,0:T(8,128)(2,1)}, u32[]{:S(2)}, u32[]{:S(2)}) collective-permute-start(bf16[128,1152]{1,0:T(8,128)(2,1)} %fusion.47), channel_id=1, source_target_pairs={{0,16},{16,0},{1,17},{17,1},{2,18},{18,2},{3,19},{19,3},{4,20},{20... | collective-permute-start | bytes 884744 | tf_op jit(solution)/shard_map/ppermute | solution.py:106
  110.8 61.5 %copy-start.31 = (bf16[128,1152]{1,0:T(8,128)(2,1)}, bf16[128,1152]{1,0:T(8,128)(2,1)S(1)}, u32[]{:S(2)}) copy-start(bf16[128,1152]{1,0:T(8,128)(2,1)S(1)} %collective-permute-done.2) | copy-start | bytes 884740
  172.3 13.9 %copy-start.62 = (f32[256,1152]{1,0:T(8,128)}, f32[256,1152]{1,0:T(8,128)S(1)}, u32[]{:S(2)}) copy-start(f32[256,1152]{1,0:T(8,128)S(1)} %convolution_add_fusion.3) | copy-start | bytes 3538948
  184.6 9.9 %collective-permute-start.5 = (bf16[128,1152]{1,0:T(8,128)(2,1)S(1)}, bf16[128,1152]{1,0:T(8,128)(2,1)S(1)}, u32[]{:S(2)}, u32[]{:S(2)}) collective-permute-start(bf16[128,1152]{1,0:T(8,128)(2,1)S(1)} %slice.300), channel_id=1, source_target_pairs={{0,16},{16,0},{1,17},{17,1},{2,18},{18,2},{3,19},{19,3},{4,20},{20... | collective-permute-start | bytes 884744 | tf_op jit(solution)/shard_map/ppermute | solution.py:106
  188.8 11.4 %collective-permute-start.3 = (bf16[128,1152]{1,0:T(8,128)(2,1)S(1)}, bf16[128,1152]{1,0:T(8,128)(2,1)S(1)}, u32[]{:S(2)}, u32[]{:S(2)}) collective-permute-start(bf16[128,1152]{1,0:T(8,128)(2,1)S(1)} %slice.301), channel_id=1, source_target_pairs={{0,16},{16,0},{1,17},{17,1},{2,18},{18,2},{3,19},{19,3},{4,20},{20... | collective-permute-start | bytes 884744 | tf_op jit(solution)/shard_map/ppermute | solution.py:106
  202.2 8.4 %collective-permute-start.6 = (bf16[128,1152]{1,0:T(8,128)(2,1)S(1)}, bf16[128,1152]{1,0:T(8,128)(2,1)S(1)}, u32[]{:S(2)}, u32[]{:S(2)}) collective-permute-start(bf16[128,1152]{1,0:T(8,128)(2,1)S(1)} %multiply_convert_fusion.5), channel_id=1, source_target_pairs={{0,16},{16,0},{1,17},{17,1},{2,18},{18,2},{3,19},{19,3},{4,20},{20... | collective-permute-start | bytes 884744 | tf_op jit(solution)/shard_map/ppermute | solution.py:106
  232.7 200.0 %reduce-scatter.9.cloned.1.call-start = ((), (), s32[]{:S(2)}) async-start(), calls=%async_computation.11 | async-start | bytes 11280384
  295.7 9.2 %collective-permute-start.7 = (bf16[128,1152]{1,0:T(8,128)(2,1)S(1)}, bf16[128,1152]{1,0:T(8,128)(2,1)S(1)}, u32[]{:S(2)}, u32[]{:S(2)}) collective-permute-start(bf16[128,1152]{1,0:T(8,128)(2,1)S(1)} %slice.299), channel_id=1, source_target_pairs={{0,16},{16,0},{1,17},{17,1},{2,18},{18,2},{3,19},{19,3},{4,20},{20... | collective-permute-start | bytes 884744 | tf_op jit(solution)/shard_map/ppermute | solution.py:106
  311.0 9.8 %all-to-all-start.2 = ((bf16[32,2,216]{2,1,0:T(2,128)(2,1)}), bf16[32,2,216]{2,1,0:T(2,128)(2,1)S(1)}, u32[]{:S(2)}, u32[]{:S(2)}) async-start(bf16[32,2,216]{2,1,0:T(2,128)(2,1)} %reshape.317), calls=%async_computation.2 | async-start | bytes 65536 | tf_op jit(solution)/shard_map/all_to_all | solution.py:242
  320.8 10.0 %all-to-all-start.4 = ((f32[32,1,504]{2,1,0:T(1,128)}), f32[32,1,504]{2,1,0:T(1,128)S(1)}, u32[]{:S(2)}, u32[]{:S(2)}) async-start(f32[32,1,504]{2,1,0:T(1,128)} %all_to_all.52), calls=%async_computation.4 | async-start | bytes 131072 | tf_op jit(solution)/shard_map/all_to_all | solution.py:265
  330.8 10.5 %all-to-all-start.3 = ((f32[16,1,1152]{2,1,0:T(1,128)}), f32[16,1,1152]{2,1,0:T(1,128)S(1)}, u32[]{:S(2)}, u32[]{:S(2)}) async-start(f32[16,1,1152]{2,1,0:T(1,128)} %copy.267), calls=%async_computation.3 | async-start | bytes 147456 | tf_op jit(solution)/shard_map/all_to_all | solution.py:248
  343.6 99.8 %collective-permute-start.8 = (bf16[72,3,576]{2,1,0:T(4,128)(2,1)S(1)}, bf16[72,3,576]{2,1,0:T(4,128)(2,1)}, u32[]{:S(2)}, u32[]{:S(2)}) collective-permute-start(bf16[72,3,576]{2,1,0:T(4,128)(2,1)S(1)} %copy.269), channel_id=1, source_target_pairs={{0,16},{16,0},{1,17},{17,1},{2,18},{18,2},{3,19},{19,3},{4,20},{20... | collective-permute-start | bytes 746504 | tf_op jit(solution)/shard_map/ppermute | solution.py:106
  438.8 11.9 %all-to-all-start.5 = ((f32[32,1,505]{2,1,0:T(1,128)}), f32[32,1,505]{2,1,0:T(1,128)}, u32[]{:S(2)}, u32[]{:S(2)}) async-start(f32[32,1,505]{2,1,0:T(1,128)} %broadcast_in_dim.121), calls=%async_computation.5 | async-start | bytes 131072 | tf_op jit(solution)/shard_map/all_to_all | solution.py:119
  447.6 33.7 %collective-permute-start.11 = (bf16[72,1,4608]{2,0,1:T(8,128)(2,1)}, bf16[72,1,4608]{2,0,1:T(8,128)(2,1)}, u32[]{:S(2)}, u32[]{:S(2)}) collective-permute-start(bf16[72,1,4608]{2,0,1:T(8,128)(2,1)} %copy.277), channel_id=1, source_target_pairs={{0,16},{16,0},{1,17},{17,1},{2,18},{18,2},{3,19},{19,3},{4,20},{20... | collective-permute-start | bytes 1990664 | tf_op jit(solution)/shard_map/ppermute | solution.py:106
  456.8 21.8 %collective-permute-start.9 = (bf16[72,1728]{1,0:T(8,128)(2,1)}, bf16[72,1728]{1,0:T(8,128)(2,1)}, u32[]{:S(2)}, u32[]{:S(2)}) collective-permute-start(bf16[72,1728]{1,0:T(8,128)(2,1)} %get-tuple-element.203), channel_id=1, source_target_pairs={{0,16},{16,0},{1,17},{17,1},{2,18},{18,2},{3,19},{19,3},{4,20},{20... | collective-permute-start | bytes 746504 | tf_op jit(solution)/shard_map/ppermute | solution.py:106
  459.4 15.0 %collective-permute-start.10 = (bf16[72,576]{0,1:T(8,128)(2,1)}, bf16[72,576]{0,1:T(8,128)(2,1)}, u32[]{:S(2)}, u32[]{:S(2)}) collective-permute-start(bf16[72,576]{0,1:T(8,128)(2,1)} %get-tuple-element.200), channel_id=1, source_target_pairs={{0,16},{16,0},{1,17},{17,1},{2,18},{18,2},{3,19},{19,3},{4,20},{20... | collective-permute-start | bytes 248840 | tf_op jit(solution)/shard_map/ppermute | solution.py:106
  464.6 35.1 %collective-permute-start.14 = (bf16[576,432]{0,1:T(8,128)(2,1)}, bf16[576,432]{0,1:T(8,128)(2,1)}, u32[]{:S(2)}, u32[]{:S(2)}) collective-permute-start(bf16[576,432]{0,1:T(8,128)(2,1)} %get-tuple-element.191), channel_id=1, source_target_pairs={{0,16},{16,0},{1,17},{17,1},{2,18},{18,2},{3,19},{19,3},{4,20},{20... | collective-permute-start | bytes 1493000 | tf_op jit(solution)/shard_map/ppermute | solution.py:106
  497.8 10.5 %collective-permute-start.12 = (bf16[72,2304]{1,0:T(8,128)(2,1)}, bf16[72,2304]{1,0:T(8,128)(2,1)}, u32[]{:S(2)}, u32[]{:S(2)}) collective-permute-start(bf16[72,2304]{1,0:T(8,128)(2,1)} %get-tuple-element.197), channel_id=1, source_target_pairs={{0,16},{16,0},{1,17},{17,1},{2,18},{18,2},{3,19},{19,3},{4,20},{20... | collective-permute-start | bytes 995336 | tf_op jit(solution)/shard_map/ppermute | solution.py:106
  508.2 8.6 %collective-permute-start.13 = (bf16[288,576]{1,0:T(8,128)(2,1)S(1)}, bf16[288,576]{1,0:T(8,128)(2,1)S(1)}, u32[]{:S(2)}, u32[]{:S(2)}) collective-permute-start(bf16[288,576]{1,0:T(8,128)(2,1)S(1)} %get-tuple-element.194), channel_id=1, source_target_pairs={{0,16},{16,0},{1,17},{17,1},{2,18},{18,2},{3,19},{19,3},{4,20},{20... | collective-permute-start | bytes 995336 | tf_op jit(solution)/shard_map/ppermute | solution.py:106
  (62 other events, 230.2 us)
Sparse Core Ops, SparseCore 0:
  10.7 68.6 all-gather.2
  82.3 87.0 all-gather.4
  232.8 76.2 reduce-scatter.6
  313.0 119.5 reduce-scatter.8
where the time goes:
time: 533 us; the launch traced here: 525 us
  waiting for transfers between devices  244 us (46%)
  other arithmetic  88.4 us (17%)
  local copies, waits for them, and re-layouts  84.7 us (16%)
  matrix products  46.5 us (9%)
  starting transfers between devices  41.5 us (8%)
  between operations  19.5 us (4%)
    unnamed x6, waiting for transfers between devices  87.4 us
    all_gather x1, waiting for transfers between devices, shards(): full_mlp = lax.all_gather(pack_mlp, 'shard', axis=0, tiled=True)  58.5 us
    unnamed x164, local copies, waits for them, and re-layouts  54.4 us
    ppermute x15, waiting for transfers between devices, swap(): return lax.ppermute(value, 'rep', couples)  46.9 us
    dot_general x23, matrix products, product(): return jnp.einsum(form, left, right, preferred_element_type=jnp.float32)  44 us
    concatenate x1, other arithmetic, shards(): jnp.concatenate(g_one + g_two, axis=1)  28.2 us
    all_gather x1, waiting for transfers between devices, shards(): full_attn = lax.all_gather(pack_attn, 'shard', axis=0, tiled=True)  21.5 us
    ppermute x15, starting transfers between devices, swap(): return lax.ppermute(value, 'rep', couples)  16.9 us
  transfers between devices with their start and end apart: 25, of which 17 were waited for; matrix products, arithmetic and copies ran while one was open for 34% of the time, Pallas kernels for 0%

commit v1 on v0

--- a/solution.py
+++ b/solution.py
@@ -15,6 +15,18 @@
 decay_rate = 0.01
 step_count = 2
 gelu_coef = 0.044715
+
+
+def review_counts_by_axis(in_array, a_name, dim_at, array_dim):
+    return jnp.concatenate(
+        jax.lax.all_to_all(
+            jnp.stack(jnp.split(in_array, jax.lax.axis_size(a_name), axis=dim_at), axis=0),
+            a_name,
+            0,
+            0,
+        ),
+        axis=array_dim,
+    )
 
 
 def product(form, left, right):
@@ -148,7 +160,7 @@
     silu_all = spread(silu_c)
     silu_group = lax.dynamic_slice_in_dim(silu_all, rank * parts, parts, 0)
     mod_cols = jnp.dot(silu_group, ada_local, preferred_element_type=jnp.float32)
-    mod = lax.all_to_all(mod_cols, "shard", split_axis=0, concat_axis=1, tiled=True) + b_ada
+    mod = review_counts_by_axis(mod_cols, "shard", 0, 1) + b_ada
     shift1, scale1, gate1, shift2, scale2, gate2 = [
         mod[:, i * width : (i + 1) * width] for i in range(6)
     ]

time: 533 us -> 534 us (level)
  local copies, waits for them, and re-layouts: 84.7 us -> 93.3 us
  waiting for transfers between devices: 244 us -> 236 us
    unnamed x164 -> x179, local copies, waits for them, and re-layouts: 54.4 us -> 63.1 us
    all_gather x1, waiting for transfers between devices: 21.5 us -> 12.9 us  [shards(): full_attn = lax.all_gather(pack_attn, 'shard', axis=0, tiled=True)]
  transfers between devices with their start and end apart: 25 -> 25, of which waited for: 17 -> 17; matrix products, arithmetic and copies ran while one was open for 34% -> 35% of each run, Pallas kernels for 0% -> 0%
where the time goes in v1:
time: 534 us; the launch traced here: 526 us
  waiting for transfers between devices  236 us (44%)
  local copies, waits for them, and re-layouts  93.3 us (17%)
  other arithmetic  88.4 us (17%)
  matrix products  46.4 us (9%)
  starting transfers between devices  41.7 us (8%)
  between operations  19.5 us (4%)
    unnamed x6, waiting for transfers between devices  87.7 us
    unnamed x179, local copies, waits for them, and re-layouts  63.1 us
    all_gather x1, waiting for transfers between devices, shards(): full_mlp = lax.all_gather(pack_mlp, 'shard', axis=0, tiled=True)  58.6 us
    ppermute x15, waiting for transfers between devices, swap(): return lax.ppermute(value, 'rep', couples)  46.5 us
    dot_general x23, matrix products, product(): return jnp.einsum(form, left, right, preferred_element_type=jnp.float32)  43.9 us
    concatenate x1, other arithmetic, shards(): jnp.concatenate(g_one + g_two, axis=1)  28.2 us
    ppermute x15, starting transfers between devices, swap(): return lax.ppermute(value, 'rep', couples)  17.1 us
    convert_element_type x5, other arithmetic, shards(): change = change.astype(jnp.bfloat16)  15 us
  transfers between devices with their start and end apart: 25, of which 17 were waited for; matrix products, arithmetic and copies ran while one was open for 35% of the time, Pallas kernels for 0%

profile of v1, /device:TPU:0, one launch (start us, length us, event | category | flops | bytes accessed | tf_op | source)
XLA Modules:
  0.0 525.7 jit_solution(714546707629774295)
XLA Ops:
  20.7 7.3 %all-to-all-start = ((bf16[32,2,576]{2,1,0:T(2,128)(2,1)}), bf16[32,2,576]{2,1,0:T(2,128)(2,1)S(1)}, u32[]{:S(2)}, u32[]{:S(2)}) async-start(bf16[32,2,576]{2,1,0:T(2,128)(2,1)} %reshape.313), calls=%async_computation | async-start | bytes 163840 | tf_op jit(solution)/shard_map/all_to_all | solution.py:131
  28.5 8.4 %all-to-all-done = bf16[32,2,576]{2,1,0:T(2,128)(2,1)S(1)} async-done(((bf16[32,2,576]{2,1,0:T(2,128)(2,1)}), bf16[32,2,576]{2,1,0:T(2,128)(2,1)S(1)}, u32[]{:S(2)}, u32[]{:S(2)}) %all-to-all-start) | async-done | bytes 73760 | tf_op jit(solution)/shard_map/all_to_all | solution.py:131
  46.9 3.7 all-to-all-start.1
  51.0 6.9 %all-to-all-done.1 = f32[16,1,432]{2,1,0:T(1,128)S(1)} async-done(((f32[16,1,432]{2,1,0:T(1,128)}), f32[16,1,432]{2,1,0:T(1,128)S(1)}, u32[]{:S(2)}, u32[]{:S(2)}) %all-to-all-start.1) | async-done | bytes 27680 | tf_op jit(solution)/shard_map/all_to_all | solution.py:22
  59.3 7.5 %collective-permute-done = bf16[128,1152]{1,0:T(8,128)(2,1)S(1)} collective-permute-done((bf16[128,1152]{1,0:T(8,128)(2,1)S(1)}, bf16[128,1152]{1,0:T(8,128)(2,1)S(1)}, u32[]{:S(2)}, u32[]{:S(2)}) %collective-permute-start) | collective-permute-done | bytes 294944 | tf_op jit(solution)/shard_map/ppermute | solution.py:118
  66.9 12.9 %all-gather.3.cloned.1.call-done = bf16[1152,2880]{1,0:T(8,128)(2,1)} async-done(((bf16[72,2880]{1,0:T(8,128)(2,1)}), bf16[1152,2880]{1,0:T(8,128)(2,1)}) %all-gather.3.cloned.1.call-update) | async-done | bytes 6635536 | tf_op jit(solution)/shard_map/all_gather | solution.py:145
  79.8 4.0 fusion.3
  89.8 6.8 %collective-permute-done.1 = bf16[2,128,576]{1,2,0:T(8,128)(2,1)S(1)} collective-permute-done((bf16[2,128,576]{1,2,0:T(8,128)(2,1)S(1)}, bf16[2,128,576]{1,2,0:T(8,128)(2,1)S(1)}, u32[]{:S(2)}, u32[]{:S(2)}) %collective-permute-start.1) | collective-permute-done | bytes 294944 | tf_op jit(solution)/shard_map/ppermute | solution.py:118
  97.4 3.3 fusion.122
  104.0 7.1 %collective-permute-done.2 = bf16[128,1152]{1,0:T(8,128)(2,1)S(1)} collective-permute-done((bf16[128,1152]{1,0:T(8,128)(2,1)S(1)}, bf16[128,1152]{1,0:T(8,128)(2,1)S(1)}, u32[]{:S(2)}, u32[]{:S(2)}) %collective-permute-start.2) | collective-permute-done | bytes 294944 | tf_op jit(solution)/shard_map/ppermute | solution.py:118
  111.1 58.6 %all-gather.5.cloned.1.call-done = bf16[1152,4608]{1,0:T(8,128)(2,1)} async-done(((bf16[72,4608]{1,0:T(8,128)(2,1)}), bf16[1152,4608]{1,0:T(8,128)(2,1)}) %all-gather.5.cloned.1.call-update) | async-done | bytes 10616848 | tf_op jit(solution)/shard_map/all_gather | solution.py:154
  172.7 3.9 convolution_add_fusion.2
  189.8 5.1 collective-permute-done.5
  195.8 4.7 collective-permute-done.3
  205.0 6.0 %collective-permute-done.6 = bf16[128,1152]{1,0:T(8,128)(2,1)S(1)} collective-permute-done((bf16[128,1152]{1,0:T(8,128)(2,1)S(1)}, bf16[128,1152]{1,0:T(8,128)(2,1)S(1)}, u32[]{:S(2)}, u32[]{:S(2)}) %collective-permute-start.6) | collective-permute-done | bytes 294944 | tf_op jit(solution)/shard_map/ppermute | solution.py:118
  224.5 8.6 %copy.285 = bf16[1152,2304]{1,0:T(8,128)(2,1)} copy(bf16[1152,2304]{0,1:T(8,128)(2,1)} %pad_maximum_fusion.1) | data formatting | bytes 10616832
  242.0 28.2 %pad_maximum_fusion = bf16[1152,4608]{0,1:T(8,128)(2,1)} fusion(bf16[1152,1152]{0,1:T(8,128)(2,1)S(1)} %convolution_convert_fusion, bf16[1152,1152]{0,1:T(8,128)(2,1)S(1)} %convolution_convert_fusion.1, bf16[1152,1152]{0,1:T(8,128)(2,1)S(1)} %convolution_convert_fusion.2, bf16[1152,1152]{0,1:T(8,128)(2,1)S(1)} %convolution_convert_fusion.3), kind=kLoop, calls=%fused_computation.1 | loop fusion | flops 42467328 | bytes 21233664 | tf_op jit(solution)/shard_map/concatenate | solution.py:212
  270.2 15.3 %copy.287 = bf16[1152,4608]{1,0:T(8,128)(2,1)} copy(bf16[1152,4608]{0,1:T(8,128)(2,1)} %pad_maximum_fusion) | data formatting | bytes 21233664
  291.0 4.0 fusion.1
  317.0 4.3 all-to-all-done.2
  325.0 6.3 %all-to-all-done.4 = f32[32,1,504]{2,1,0:T(1,128)S(1)} async-done(((f32[32,1,504]{2,1,0:T(1,128)}), f32[32,1,504]{2,1,0:T(1,128)S(1)}, u32[]{:S(2)}, u32[]{:S(2)}) %all-to-all-start.4) | async-done | bytes 64544 | tf_op jit(solution)/shard_map/all_to_all | solution.py:277
  331.2 3.5 all-to-all-start.3
  338.1 3.5 all-to-all-done.3
  345.7 87.6 %reduce-scatter.9.cloned.1.call-done = bf16[72,4608]{1,0:T(8,128)(2,1)} async-done(((bf16[1152,4608]{1,0:T(8,128)(2,1)}), bf16[72,4608]{1,0:T(8,128)(2,1)}) %reduce-scatter.9.cloned.1.call-update) | async-done | bytes 663568
  439.5 4.6 all-to-all-start.5
  454.4 3.1 multiply_convert_fusion.6
  461.4 3.9 multiply_convert_fusion.2
  471.8 3.3 collective-permute-done.10
  490.6 5.0 reshape.285
  500.4 3.5 convert_add_fusion
  505.7 3.2 multiply_convert_fusion.3
  511.6 5.9 %collective-permute-done.13 = bf16[288,576]{1,0:T(8,128)(2,1)S(1)} collective-permute-done((bf16[288,576]{1,0:T(8,128)(2,1)S(1)}, bf16[288,576]{1,0:T(8,128)(2,1)S(1)}, u32[]{:S(2)}, u32[]{:S(2)}) %collective-permute-start.13) | collective-permute-done | bytes 331808 | tf_op jit(solution)/shard_map/ppermute | solution.py:118
  (363 shorter events, 166.2 us)
Async XLA Ops:
  7.2 72.6 %all-gather.3.cloned.1.call-start = ((), (), s32[]{:S(2)}) async-start(), calls=%async_computation.8 | async-start | bytes 7206912 | tf_op jit(solution)/shard_map/all_gather | solution.py:145
  10.3 159.4 %all-gather.5.cloned.1.call-start = ((), (), s32[]{:S(2)}) async-start(), calls=%async_computation.9 | async-start | bytes 11280384 | tf_op jit(solution)/shard_map/all_gather | solution.py:154
  16.6 20.6 %copy-start = (f32[1152,432]{0,1:T(8,128)S(1)}, f32[1152,432]{0,1:T(8,128)}, u32[]{:S(2)}) copy-start(f32[1152,432]{0,1:T(8,128)} %param.30) | copy-start | bytes 5971972
  20.7 16.2 %all-to-all-start = ((bf16[32,2,576]{2,1,0:T(2,128)(2,1)}), bf16[32,2,576]{2,1,0:T(2,128)(2,1)S(1)}, u32[]{:S(2)}, u32[]{:S(2)}) async-start(bf16[32,2,576]{2,1,0:T(2,128)(2,1)} %reshape.313), calls=%async_computation | async-start | bytes 163840 | tf_op jit(solution)/shard_map/all_to_all | solution.py:131
  28.2 29.9 %copy-start.55 = (f32[128]{0:T(128)}, f32[128]{0:T(128)S(1)}, u32[]{:S(2)}) copy-start(f32[128]{0:T(128)S(1)} %broadcast_multiply_fusion.5) | copy-start | bytes 1540
  37.1 13.8 %copy-start.35 = (bf16[32,1,1152]{2,1,0:T(2,128)(2,1)}, bf16[32,1,1152]{2,1,0:T(2,128)(2,1)S(1)}, u32[]{:S(2)}) copy-start(bf16[32,1,1152]{2,1,0:T(2,128)(2,1)S(1)} %reshape.314) | copy-start | bytes 221188
  46.9 11.0 %all-to-all-start.1 = ((f32[16,1,432]{2,1,0:T(1,128)}), f32[16,1,432]{2,1,0:T(1,128)S(1)}, u32[]{:S(2)}, u32[]{:S(2)}) async-start(f32[16,1,432]{2,1,0:T(1,128)} %constant_dynamic-update-slice_fusion), calls=%async_computation.1 | async-start | bytes 65536 | tf_op jit(solution)/shard_map/all_to_all | solution.py:22
  50.6 291.8 %reduce-scatter.7.cloned.1.call-start = ((), (), s32[]{:S(2)}) async-start(), calls=%async_computation.10 | async-start | bytes 5640192
  58.4 25.3 %copy-start.19 = (bf16[128,1152]{1,0:T(8,128)(2,1)}, bf16[128,1152]{1,0:T(8,128)(2,1)S(1)}, u32[]{:S(2)}) copy-start(bf16[128,1152]{1,0:T(8,128)(2,1)S(1)} %fusion.50) | copy-start | bytes 884740
  58.4 8.4 %collective-permute-start = (bf16[128,1152]{1,0:T(8,128)(2,1)S(1)}, bf16[128,1152]{1,0:T(8,128)(2,1)S(1)}, u32[]{:S(2)}, u32[]{:S(2)}) collective-permute-start(bf16[128,1152]{1,0:T(8,128)(2,1)S(1)} %fusion.50), channel_id=1, source_target_pairs={{0,16},{16,0},{1,17},{17,1},{2,18},{18,2},{3,19},{19,3},{4,20},{20... | collective-permute-start | bytes 884744 | tf_op jit(solution)/shard_map/ppermute | solution.py:118
  87.4 9.2 %collective-permute-start.1 = (bf16[2,128,576]{1,2,0:T(8,128)(2,1)S(1)}, bf16[2,128,576]{1,2,0:T(8,128)(2,1)S(1)}, u32[]{:S(2)}, u32[]{:S(2)}) collective-permute-start(bf16[2,128,576]{1,2,0:T(8,128)(2,1)S(1)} %bitcast.218), channel_id=1, source_target_pairs={{0,16},{16,0},{1,17},{17,1},{2,18},{18,2},{3,19},{19,3},{4,20},{20... | collective-permute-start | bytes 884744 | tf_op jit(solution)/shard_map/ppermute | solution.py:118
  101.2 71.5 %copy-start.10 = (bf16[128,1152]{1,0:T(8,128)(2,1)}, bf16[128,1152]{1,0:T(8,128)(2,1)S(1)}, u32[]{:S(2)}) copy-start(bf16[128,1152]{1,0:T(8,128)(2,1)S(1)} %add_convert_fusion) | copy-start | bytes 884740
  101.2 9.9 %collective-permute-start.2 = (bf16[128,1152]{1,0:T(8,128)(2,1)S(1)}, bf16[128,1152]{1,0:T(8,128)(2,1)S(1)}, u32[]{:S(2)}, u32[]{:S(2)}) collective-permute-start(bf16[128,1152]{1,0:T(8,128)(2,1)S(1)} %add_convert_fusion), channel_id=1, source_target_pairs={{0,16},{16,0},{1,17},{17,1},{2,18},{18,2},{3,19},{19,3},{4,20},{20... | collective-permute-start | bytes 884744 | tf_op jit(solution)/shard_map/ppermute | solution.py:118
  103.5 73.1 %collective-permute-start.4 = (bf16[128,1152]{1,0:T(8,128)(2,1)}, bf16[128,1152]{1,0:T(8,128)(2,1)}, u32[]{:S(2)}, u32[]{:S(2)}) collective-permute-start(bf16[128,1152]{1,0:T(8,128)(2,1)} %fusion.47), channel_id=1, source_target_pairs={{0,16},{16,0},{1,17},{17,1},{2,18},{18,2},{3,19},{19,3},{4,20},{20... | collective-permute-start | bytes 884744 | tf_op jit(solution)/shard_map/ppermute | solution.py:118
  111.1 61.5 %copy-start.31 = (bf16[128,1152]{1,0:T(8,128)(2,1)}, bf16[128,1152]{1,0:T(8,128)(2,1)S(1)}, u32[]{:S(2)}) copy-start(bf16[128,1152]{1,0:T(8,128)(2,1)S(1)} %collective-permute-done.2) | copy-start | bytes 884740
  172.7 13.9 %copy-start.62 = (f32[256,1152]{1,0:T(8,128)}, f32[256,1152]{1,0:T(8,128)S(1)}, u32[]{:S(2)}) copy-start(f32[256,1152]{1,0:T(8,128)S(1)} %convolution_add_fusion.3) | copy-start | bytes 3538948
  185.0 9.9 %collective-permute-start.5 = (bf16[128,1152]{1,0:T(8,128)(2,1)S(1)}, bf16[128,1152]{1,0:T(8,128)(2,1)S(1)}, u32[]{:S(2)}, u32[]{:S(2)}) collective-permute-start(bf16[128,1152]{1,0:T(8,128)(2,1)S(1)} %slice.300), channel_id=1, source_target_pairs={{0,16},{16,0},{1,17},{17,1},{2,18},{18,2},{3,19},{19,3},{4,20},{20... | collective-permute-start | bytes 884744 | tf_op jit(solution)/shard_map/ppermute | solution.py:118
  189.2 11.4 %collective-permute-start.3 = (bf16[128,1152]{1,0:T(8,128)(2,1)S(1)}, bf16[128,1152]{1,0:T(8,128)(2,1)S(1)}, u32[]{:S(2)}, u32[]{:S(2)}) collective-permute-start(bf16[128,1152]{1,0:T(8,128)(2,1)S(1)} %slice.301), channel_id=1, source_target_pairs={{0,16},{16,0},{1,17},{17,1},{2,18},{18,2},{3,19},{19,3},{4,20},{20... | collective-permute-start | bytes 884744 | tf_op jit(solution)/shard_map/ppermute | solution.py:118
  202.6 8.4 %collective-permute-start.6 = (bf16[128,1152]{1,0:T(8,128)(2,1)S(1)}, bf16[128,1152]{1,0:T(8,128)(2,1)S(1)}, u32[]{:S(2)}, u32[]{:S(2)}) collective-permute-start(bf16[128,1152]{1,0:T(8,128)(2,1)S(1)} %multiply_convert_fusion.5), channel_id=1, source_target_pairs={{0,16},{16,0},{1,17},{17,1},{2,18},{18,2},{3,19},{19,3},{4,20},{20... | collective-permute-start | bytes 884744 | tf_op jit(solution)/shard_map/ppermute | solution.py:118
  233.1 200.2 %reduce-scatter.9.cloned.1.call-start = ((), (), s32[]{:S(2)}) async-start(), calls=%async_computation.11 | async-start | bytes 11280384
  296.0 9.3 %collective-permute-start.7 = (bf16[128,1152]{1,0:T(8,128)(2,1)S(1)}, bf16[128,1152]{1,0:T(8,128)(2,1)S(1)}, u32[]{:S(2)}, u32[]{:S(2)}) collective-permute-start(bf16[128,1152]{1,0:T(8,128)(2,1)S(1)} %slice.299), channel_id=1, source_target_pairs={{0,16},{16,0},{1,17},{17,1},{2,18},{18,2},{3,19},{19,3},{4,20},{20... | collective-permute-start | bytes 884744 | tf_op jit(solution)/shard_map/ppermute | solution.py:118
  311.4 9.8 %all-to-all-start.2 = ((bf16[32,2,216]{2,1,0:T(2,128)(2,1)}), bf16[32,2,216]{2,1,0:T(2,128)(2,1)S(1)}, u32[]{:S(2)}, u32[]{:S(2)}) async-start(bf16[32,2,216]{2,1,0:T(2,128)(2,1)} %reshape.315), calls=%async_computation.2 | async-start | bytes 65536 | tf_op jit(solution)/shard_map/all_to_all | solution.py:254
  321.2 10.0 %all-to-all-start.4 = ((f32[32,1,504]{2,1,0:T(1,128)}), f32[32,1,504]{2,1,0:T(1,128)S(1)}, u32[]{:S(2)}, u32[]{:S(2)}) async-start(f32[32,1,504]{2,1,0:T(1,128)} %all_to_all.41), calls=%async_computation.4 | async-start | bytes 131072 | tf_op jit(solution)/shard_map/all_to_all | solution.py:277
  331.2 10.5 %all-to-all-start.3 = ((f32[16,1,1152]{2,1,0:T(1,128)}), f32[16,1,1152]{2,1,0:T(1,128)S(1)}, u32[]{:S(2)}, u32[]{:S(2)}) async-start(f32[16,1,1152]{2,1,0:T(1,128)} %copy.262), calls=%async_computation.3 | async-start | bytes 147456 | tf_op jit(solution)/shard_map/all_to_all | solution.py:260
  344.1 100.0 %collective-permute-start.8 = (bf16[72,3,576]{2,1,0:T(4,128)(2,1)S(1)}, bf16[72,3,576]{2,1,0:T(4,128)(2,1)}, u32[]{:S(2)}, u32[]{:S(2)}) collective-permute-start(bf16[72,3,576]{2,1,0:T(4,128)(2,1)S(1)} %copy.264), channel_id=1, source_target_pairs={{0,16},{16,0},{1,17},{17,1},{2,18},{18,2},{3,19},{19,3},{4,20},{20... | collective-permute-start | bytes 746504 | tf_op jit(solution)/shard_map/ppermute | solution.py:118
  439.5 12.0 %all-to-all-start.5 = ((f32[32,1,505]{2,1,0:T(1,128)}), f32[32,1,505]{2,1,0:T(1,128)}, u32[]{:S(2)}, u32[]{:S(2)}) async-start(f32[32,1,505]{2,1,0:T(1,128)} %broadcast_in_dim.121), calls=%async_computation.5 | async-start | bytes 131072 | tf_op jit(solution)/shard_map/all_to_all | solution.py:131
  448.3 33.7 %collective-permute-start.11 = (bf16[72,1,4608]{2,0,1:T(8,128)(2,1)}, bf16[72,1,4608]{2,0,1:T(8,128)(2,1)}, u32[]{:S(2)}, u32[]{:S(2)}) collective-permute-start(bf16[72,1,4608]{2,0,1:T(8,128)(2,1)} %copy.272), channel_id=1, source_target_pairs={{0,16},{16,0},{1,17},{17,1},{2,18},{18,2},{3,19},{19,3},{4,20},{20... | collective-permute-start | bytes 1990664 | tf_op jit(solution)/shard_map/ppermute | solution.py:118
  457.5 21.8 %collective-permute-start.9 = (bf16[72,1728]{1,0:T(8,128)(2,1)}, bf16[72,1728]{1,0:T(8,128)(2,1)}, u32[]{:S(2)}, u32[]{:S(2)}) collective-permute-start(bf16[72,1728]{1,0:T(8,128)(2,1)} %get-tuple-element.203), channel_id=1, source_target_pairs={{0,16},{16,0},{1,17},{17,1},{2,18},{18,2},{3,19},{19,3},{4,20},{20... | collective-permute-start | bytes 746504 | tf_op jit(solution)/shard_map/ppermute | solution.py:118
  460.1 15.0 %collective-permute-start.10 = (bf16[72,576]{0,1:T(8,128)(2,1)}, bf16[72,576]{0,1:T(8,128)(2,1)}, u32[]{:S(2)}, u32[]{:S(2)}) collective-permute-start(bf16[72,576]{0,1:T(8,128)(2,1)} %get-tuple-element.200), channel_id=1, source_target_pairs={{0,16},{16,0},{1,17},{17,1},{2,18},{18,2},{3,19},{19,3},{4,20},{20... | collective-permute-start | bytes 248840 | tf_op jit(solution)/shard_map/ppermute | solution.py:118
  465.3 35.1 %collective-permute-start.14 = (bf16[576,432]{0,1:T(8,128)(2,1)}, bf16[576,432]{0,1:T(8,128)(2,1)}, u32[]{:S(2)}, u32[]{:S(2)}) collective-permute-start(bf16[576,432]{0,1:T(8,128)(2,1)} %get-tuple-element.191), channel_id=1, source_target_pairs={{0,16},{16,0},{1,17},{17,1},{2,18},{18,2},{3,19},{19,3},{4,20},{20... | collective-permute-start | bytes 1493000 | tf_op jit(solution)/shard_map/ppermute | solution.py:118
  498.5 10.5 %collective-permute-start.12 = (bf16[72,2304]{1,0:T(8,128)(2,1)}, bf16[72,2304]{1,0:T(8,128)(2,1)}, u32[]{:S(2)}, u32[]{:S(2)}) collective-permute-start(bf16[72,2304]{1,0:T(8,128)(2,1)} %get-tuple-element.197), channel_id=1, source_target_pairs={{0,16},{16,0},{1,17},{17,1},{2,18},{18,2},{3,19},{19,3},{4,20},{20... | collective-permute-start | bytes 995336 | tf_op jit(solution)/shard_map/ppermute | solution.py:118
  508.9 8.6 %collective-permute-start.13 = (bf16[288,576]{1,0:T(8,128)(2,1)S(1)}, bf16[288,576]{1,0:T(8,128)(2,1)S(1)}, u32[]{:S(2)}, u32[]{:S(2)}) collective-permute-start(bf16[288,576]{1,0:T(8,128)(2,1)S(1)} %get-tuple-element.194), channel_id=1, source_target_pairs={{0,16},{16,0},{1,17},{17,1},{2,18},{18,2},{3,19},{19,3},{4,20},{20... | collective-permute-start | bytes 995336 | tf_op jit(solution)/shard_map/ppermute | solution.py:118
  (62 other events, 247.2 us)
Sparse Core Ops, SparseCore 0:
  10.7 69.0 all-gather.2
  82.6 87.0 all-gather.4
  233.2 76.3 reduce-scatter.6
  313.5 119.7 reduce-scatter.8
